TPU v7x, 256 devices: a whole 4x4x8 slice. The times are simulated.
256 devices in a mesh: dp: 32 (over y, x, core), ka: 8 (over z).
Axes of the slice: x: 4, y: 4, z: 8, core: 2. Of those that a mesh axis runs over, the one named last changes fastest.
Arguments:
- feats: bfloat16 [65536, 256], P('dp'), may hold values from -6 to 6
- coords: float32 [3, 65536], P(None, 'dp'), may hold values from 0 to 1
- cell_ids: int32 [32, 2048], P('dp'), may hold values from 0 to 7, never falling along the last dimension, each value on 1 to 1024 neighbouring positions
- recip: float32 [32, 8, 9], P('dp'), may hold values from 0.05 to 0.35
- kvec: int32 [3, 1024], P(None, 'ka'), may hold values from -4 to 4
- w_in: bfloat16 [256, 256], replicated, may hold values from -0.375 to 0.375
- w_out: bfloat16 [256, 256], replicated, may hold values from -0.375 to 0.375
- kfilt: float32 [1024, 256], P('ka'), may hold values from -3 to 3
- spread: float32 [256], replicated, may hold values from 0.02 to 0.5
- cotan: bfloat16 [65536, 256], P('dp'), may hold values from -6 to 6
Outputs:
- mixed: bfloat16 [65536, 256], P('dp')
- feat_grad: bfloat16 [65536, 256], P('dp')
- grad_w_in: float32 [256, 256], replicated
- grad_w_out: float32 [256, 256], replicated
- grad_kfilt: float32 [1024, 256], P('ka')
Inputs may be any that keep to these rules, and one draw needn't show every extreme that they name: `cell_ids`: within each row, cell numbers never fall; each of the 8 cells holds 1 to 1024 atoms, and one holds exactly 1024.
All inputs are finite; a program needn't handle non-finite values.
Results may differ from a plain program's by a relative error of at most 0.0056.
The roundings to bfloat16 on the way count: a program that leaves them out, or rounds other values in their place, can miss the bound.
Values may be sent and summed in bfloat16 or wider, within the bound.
A program may use at most 64 MiB of HBM per device.

v0:
```python
import functools

import jax
import jax.numpy as jnp
from jax import lax
from jax.experimental import pallas as pl
from jax.experimental.pallas import tpu as pltpu
from jax.sharding import PartitionSpec as P

MESH = pl.DeviceIdType.MESH
F32, BF16 = jnp.float32, jnp.bfloat16
NT = (((1,), (1,)), ((), ()))
TN = (((0,), (0,)), ((), ()))
GATHER_VMEM, REDUCE_VMEM = 30 << 20, 30 << 20
POINTS = 384
DEPTHS = (256, 384, 512, 768, 1152)
HEIGHTS = (96, 160, 224, 320, 528, 784, 1040)
COS = (0.9999992251396179, -19.738981246948242, 64.92865753173828, -85.27162170410156, 58.79049301147461, -21.07110595703125)
SIN = (6.283185005187988, -41.341590881347656, 81.59994506835938, -76.61447143554688, 41.3428840637207, -12.471243858337402)


def poly(coefs, s):
    total = coefs[-1] * s + coefs[-2]
    for c in coefs[-3::-1]:
        total = total * s + c
    return total


def mm(a, b):
    return jnp.dot(a, b, preferred_element_type=F32)


def mm_nt(a, b):
    return lax.dot_general(a, b, NT, preferred_element_type=F32)


def mm_tn(a, b):
    return lax.dot_general(a, b, TN, preferred_element_type=F32)


def lattice(shape, axis):
    n = lax.broadcasted_iota(jnp.int32, shape, axis).astype(F32) + 364.0
    i = jnp.floor((n + 0.5) * (1.0 / 81.0))
    rest = n - 81.0 * i
    j = jnp.floor((rest + 0.5) * (1.0 / 9.0))
    return i - 4.0, j - 4.0, rest - 9.0 * j - 4.0


def point_of(k):
    return jnp.abs(81.0 * k[0:1] + 9.0 * k[1:2] + k[2:3])


def gather_kernel(
    n_ka, feats_in, coords_in, cells_in, recip_in, kvec_in, w_in_in, kfilt_in, spread_in, cotan_in, w_out_in,
    cs, ct, proj, back, shapes, kf, meta,
    feats, coords, own_cells, recip, kvec, w_in, kfilt, spread, cotan, w_out,
    high, low, loads, send, recv, p_send, p_recv,
):
    me, dp = lax.axis_index("ka"), lax.axis_index("dp")
    right, left = lax.rem(me + 1, n_ka), lax.rem(me + n_ka - 1, n_ka)
    core = lax.rem(dp, 2)
    twin = dp + 1 - 2 * core
    barrier = pltpu.get_barrier_semaphore()
    for peer in (left, right):
        pl.semaphore_signal(barrier, inc=1, device_id={"ka": peer}, device_id_type=MESH)
    pl.semaphore_signal(barrier, inc=1, device_id={"dp": twin}, device_id_type=MESH)
    pairs = (
        (kfilt_in, kfilt), (kvec_in, kvec), (coords_in, coords), (cells_in, own_cells), (w_in_in, w_in),
        (feats_in, feats), (recip_in, recip), (spread_in, spread), (w_out_in, w_out), (cotan_in, cotan),
    )
    loading = [pltpu.make_async_copy(a, b, loads.at[i]) for i, (a, b) in enumerate(pairs)]
    for c in loading:
        c.start()
    depth, chan = kfilt.shape
    part = depth // 2
    atoms = cs.shape[1]
    loading[0].wait()
    loading[1].wait()
    first = kfilt[...].astype(BF16)
    second = (kfilt[...] - first.astype(F32)).astype(BF16)
    kpad = jnp.concatenate([kvec[...].astype(F32), jnp.zeros((13, depth), F32)], axis=0)
    for h in range(2):
        rows = slice(h * part, (h + 1) * part)
        high[me, h, 0:part, :] = first[rows]
        low[me, h] = second[rows]
        k = kpad[:, rows]
        high[me, h, part:part + 16, :] = jnp.concatenate([k, k, k, k], axis=1).astype(BF16)
    pl.semaphore_wait(barrier, 3)

    hops = (n_ka // 2, n_ka - 1 - n_ka // 2)
    halves = (high, low)

    def hop(half, way, step):
        slot = lax.rem(me - step + n_ka, n_ka) if way == 0 else lax.rem(me + step, n_ka)
        ref = halves[half].at[slot, core]
        return pltpu.make_async_remote_copy(
            src_ref=ref, dst_ref=ref, send_sem=send.at[half, way, step], recv_sem=recv.at[half, way, step],
            device_id={"ka": right if way == 0 else left}, device_id_type=MESH,
        )

    def share(half, way, step):
        slot = lax.rem(me - step - 1 + n_ka, n_ka) if way == 0 else lax.rem(me + step + 1, n_ka)
        ref = halves[half].at[slot, core]
        return pltpu.make_async_remote_copy(
            src_ref=ref, dst_ref=ref, send_sem=p_send.at[half, way, step], recv_sem=p_recv.at[half, way, step],
            device_id={"dp": twin}, device_id_type=MESH,
        )

    def trig(i):
        at = pl.multiple_of(i * 16, 16)
        n = (lax.broadcasted_iota(jnp.int32, (16, 1), 0) + (at + 364)).astype(F32)
        kx = jnp.floor((n + 0.5) * (1.0 / 81.0))
        rest = n - 81.0 * kx
        ky = jnp.floor((rest + 0.5) * (1.0 / 9.0))
        kz = rest - 9.0 * ky - 4.0
        kx, ky = kx - 4.0, ky - 4.0
        for lane in range(0, atoms, 512):
            here = pl.ds(lane, 512)
            turn = (coords[0:1, here] * kx + coords[1:2, here] * ky) + coords[2:3, here] * kz
            turn = turn - jnp.round(turn)
            s = turn * turn
            cs[pl.ds(at, 16), here] = poly(COS, s).astype(BF16)
            cs[pl.ds(POINTS + at, 16), here] = (turn * poly(SIN, s)).astype(BF16)

    chunks = POINTS // 16
    split = chunks // 2

    def envelope():
        loading[3].wait()
        loading[6].wait()
        loading[7].wait()
        n_cells = recip.shape[1]
        own = own_cells[...]
        lane = lax.broadcasted_iota(jnp.int32, (1, 128), 1)
        info = jnp.zeros((1, 128), jnp.int32)
        kx, ky, kz = lattice((1, POINTS), 1)
        b = recip[0]
        q = jnp.zeros((n_cells, POINTS), F32)
        for r in range(3):
            dot = (b[:, 3 * r:3 * r + 1] * kx + b[:, 3 * r + 1:3 * r + 2] * ky) + b[:, 3 * r + 2:3 * r + 3] * kz
            q = q + dot * dot
        q = jnp.concatenate([q] + [jnp.zeros((128 - n_cells, POINTS), F32)], axis=0).T
        for i in range(n_cells):
            count = jnp.sum((own == i).astype(F32), axis=1, keepdims=True)
            before = jnp.sum((own < i).astype(F32), axis=1, keepdims=True)
            info = jnp.where(lane == i, before.astype(jnp.int32), info)
            info = jnp.where(lane == 8 + i, count.astype(jnp.int32), info)
            shapes[i] = jnp.exp(-(q[:, i:i + 1] * spread[...])) * (1.0 / count)
        meta[...] = info

    def stage(step):
        if step == 0:
            loading[4].wait()
            loading[5].wait()
            proj[...] = mm(feats[...], w_in[...]).astype(BF16)
            loading[2].wait()
            pl.loop(0, split)(trig)
        elif step == 1:
            pl.loop(split, chunks)(trig)
        elif step == 2:
            envelope()
            loading[8].wait()
            loading[9].wait()
            back[...] = mm_nt(cotan[...], w_out[...])
        else:
            for p in range(0, 2 * POINTS, 256):
                for a in range(0, atoms, 256):
                    ct[a:a + 256, p:p + 256] = cs[p:p + 256, a:a + 256].T

    pending, shared = [], []

    def ways(step):
        return [way for way in (0, 1) if 0 <= step < hops[way]]

    for step in range(hops[0] + 1):
        for half in (0, 1):
            for way in ways(step - 1):
                hop(half, way, step - 1).wait_recv()
            for way in ways(step):
                c = hop(half, way, step)
                c.start()
                pending.append(c)
            for way in ways(step - 1):
                c = share(half, way, step - 1)
                c.start()
                shared.append(c)
        if step < hops[0]:
            stage(step)
    for c in shared:
        c.wait_recv()
    point = lax.broadcasted_iota(jnp.int32, (POINTS, 2 * depth), 0).astype(F32)
    total = jnp.zeros((POINTS, chan), F32)
    for z in range(n_ka):
        k = jnp.concatenate([high[z, h, part:part + 16, 0:depth] for h in (0, 1)], axis=1).astype(F32)
        hot = (point == point_of(k)).astype(BF16)
        terms = jnp.concatenate([high[z, 0, 0:part, :], low[z, 0], high[z, 1, 0:part, :], low[z, 1]], axis=0)
        total = total + mm(hot, terms)
    kf[...] = total
    for c in pending + shared:
        c.wait_send()


def cell_kernel(meta, cs, ct, proj, back, shapes, kf, act, upd, rsum, pull, push, grad):
    atoms = cs.shape[1]
    half, other = pl.ds(0, POINTS), pl.ds(POINTS, POINTS)

    def windows(i, unit, sizes, run):
        off, n = meta[0, i], meta[0, 8 + i]
        base = lax.div(off, unit) * unit
        span = off + n - base
        low = 0
        for size in sizes:
            @pl.when((span > low) & (span <= size))
            def _():
                start = pl.multiple_of(jnp.minimum(base, atoms - size), unit)
                row = lax.broadcasted_iota(jnp.int32, (size, 1), 0) + start
                run(pl.ds(start, size), (row >= off) & (row < off + n))
            low = size

    def factors(source, target, i):
        def run(here, inside):
            picked = jnp.where(inside, source[here, :].astype(F32), 0.0).astype(BF16)
            target[...] = mm(cs[:, here], picked)
        windows(i, 128, DEPTHS, run)

    def fields(filt, terms, i, use):
        weights = jnp.concatenate([(filt * terms[half]).astype(BF16), (filt * terms[other]).astype(BF16)], axis=0)

        def run(here, inside):
            use(here, inside, mm(ct[here, :], weights))
        windows(i, 16, HEIGHTS, run)

    def keep(target, here, inside, new):
        target[here, :] = jnp.where(inside, new, target[here, :].astype(F32)).astype(BF16)

    def forward(here, inside, m):
        s = 0.5 * jnp.tanh(0.5 * m) + 0.5
        keep(act, here, inside, m * s)
        keep(grad, here, inside, back[here, :] * (s * (1.0 + m * (1.0 - s))))

    rsum[...] = jnp.zeros_like(rsum)

    @pl.loop(0, shapes.shape[0])
    def _(i):
        factors(proj, push, i)
        fields(shapes[i] * kf[...], push, i, forward)
        factors(grad, pull, i)
        shape = shapes[i]
        rsum[...] += shape * (push[half] * pull[half] + push[other] * pull[other])
        fields(shape * kf[...], pull, i, functools.partial(keep, upd))


def reduce_kernel(
    n_dp, n_ka, mean_weights, mean_filter, act, upd, rsum, feats_in, cotan_in, w_in_in, w_out_in, kvec_in,
    mixed, feat_grad, grad_in, grad_out, grad_filt,
    feats, cotan, w_in, w_out, kvec, raw, landed, gath, squares, sq_landed, sq_gath,
    loads, s_send, s_recv, g_send, g_recv, z_send, z_recv, q_send, q_recv,
):
    pairs = ((cotan_in, cotan), (feats_in, feats), (kvec_in, kvec), (w_out_in, w_out), (w_in_in, w_in))
    loading = [pltpu.make_async_copy(a, b, loads.at[i]) for i, (a, b) in enumerate(pairs)]
    for c in loading:
        c.start()
    me, ka = lax.axis_index("dp"), lax.axis_index("ka")
    chan = grad_in.shape[0]
    height = chan // n_dp
    barrier = pltpu.get_barrier_semaphore()

    def peer(i):
        return lax.rem(me + i, n_dp)

    @pl.loop(1, n_dp)
    def _(i):
        pl.semaphore_signal(barrier, inc=1, device_id={"dp": peer(i)}, device_id_type=MESH)

    @pl.loop(1, n_ka)
    def _(i):
        pl.semaphore_signal(barrier, inc=1, device_id={"ka": lax.rem(ka + i, n_ka)}, device_id_type=MESH)

    atoms, depth = act.shape[0], kvec.shape[1]
    for c in loading:
        c.wait()
    raw[:, :, 0:chan] = mm_tn(act[...], cotan[...]).reshape(n_dp, height, chan).astype(BF16)
    raw[:, :, chan:2 * chan] = mm_tn(feats[...], upd[...]).reshape(n_dp, height, chan).astype(BF16)
    point = lax.broadcasted_iota(jnp.int32, (POINTS, depth), 0).astype(F32)
    hot = (point == point_of(kvec[...].astype(F32))).astype(BF16).T
    rest = rsum[...]
    own = jnp.zeros((depth, chan), F32)
    for _ in range(3):
        piece = rest.astype(BF16)
        own = own + mm(hot, piece)
        rest = rest - piece.astype(F32)
    own = jnp.concatenate([own[:, 0:chan // 2], own[:, chan // 2:]], axis=0)
    raw[:, :, 2 * chan:] = own.reshape(n_dp, height, chan // 2).astype(BF16)
    pl.semaphore_wait(barrier, n_dp - 1 + n_ka - 1)

    def scatter(i):
        return pltpu.make_async_remote_copy(
            src_ref=raw.at[peer(i)], dst_ref=landed.at[i - 1], send_sem=s_send.at[i - 1], recv_sem=s_recv.at[i - 1],
            device_id={"dp": peer(i)}, device_id_type=MESH,
        )

    def gather(i):
        return pltpu.make_async_remote_copy(
            src_ref=gath.at[me], dst_ref=gath.at[me], send_sem=g_send.at[i - 1], recv_sem=g_recv.at[i - 1],
            device_id={"dp": peer(i)}, device_id_type=MESH,
        )

    def across(i):
        return pltpu.make_async_remote_copy(
            src_ref=squares, dst_ref=sq_landed.at[i - 1], send_sem=z_send.at[i - 1], recv_sem=z_recv.at[i - 1],
            device_id={"ka": lax.rem(ka + i, n_ka)}, device_id_type=MESH,
        )

    def gather_sq(i):
        return pltpu.make_async_remote_copy(
            src_ref=sq_gath.at[me], dst_ref=sq_gath.at[me], send_sem=q_send.at[i - 1], recv_sem=q_recv.at[i - 1],
            device_id={"dp": peer(i)}, device_id_type=MESH,
        )

    def each(copy, act, n):
        @pl.loop(1, n)
        def _(i):
            act(copy(i))

    each(scatter, lambda c: c.start(), n_dp)
    for a in range(0, atoms, 512):
        mixed[a:a + 512, :] = (feats[a:a + 512, :].astype(F32) + mm(act[a:a + 512, :], w_out[...])).astype(BF16)
    each(scatter, lambda c: c.wait_recv(), n_dp)
    total = raw[me].astype(F32)
    for i in range(n_dp - 1):
        total = total + landed[i].astype(F32)
    gath[me] = total.astype(BF16)
    each(gather, lambda c: c.start(), n_dp)
    tail = total[:, 2 * chan:]
    squares[...] = tail * tail
    each(across, lambda c: c.start(), n_ka)
    for a in range(0, atoms, 512):
        feat_grad[a:a + 512, :] = (cotan[a:a + 512, :].astype(F32) + mm_nt(upd[a:a + 512, :], w_in[...])).astype(BF16)
    each(across, lambda c: c.wait_recv(), n_ka)
    added = squares[...]
    for i in range(n_ka - 1):
        added = added + sq_landed[i]
    sq_gath[me] = added
    each(gather_sq, lambda c: c.start(), n_dp)
    each(gather, lambda c: c.wait_recv(), n_dp)
    everything = gath[...].astype(F32).reshape(chan, gath.shape[2])
    weights = everything[:, 0:2 * chan]
    scale = lax.rsqrt(jnp.sum(weights * weights, axis=(0, 1), keepdims=True) * mean_weights + 1e-06)
    grad_out[...] = everything[:, 0:chan] * scale
    grad_in[...] = everything[:, chan:2 * chan] * scale
    each(gather_sq, lambda c: c.wait_recv(), n_dp)
    summed = sq_gath[...].reshape(n_dp * height, sq_gath.shape[2])
    scale = lax.rsqrt(jnp.sum(summed, axis=(0, 1), keepdims=True) * mean_filter + 1e-06)
    tail = everything[:, 2 * chan:] * scale
    grad_filt[...] = jnp.concatenate([tail[0:depth], tail[depth:]], axis=1)
    each(scatter, lambda c: c.wait_send(), n_dp)
    each(gather, lambda c: c.wait_send(), n_dp)
    each(across, lambda c: c.wait_send(), n_ka)
    each(gather_sq, lambda c: c.wait_send(), n_dp)


def put_kernel(*refs):
    n = (len(refs) - 1) // 2
    copies = [pltpu.make_async_copy(refs[i], refs[n + i], refs[-1].at[i]) for i in range(n)]
    for c in copies:
        c.start()
    for c in copies:
        c.wait()


def solution(mesh):
    n_dp, n_ka = mesh.shape["dp"], mesh.shape["ka"]
    vmem = pl.BlockSpec(memory_space=pltpu.VMEM)
    smem = pl.BlockSpec(memory_space=pltpu.SMEM)
    hbm = pl.BlockSpec(memory_space=pltpu.HBM)
    dma = pltpu.SemaphoreType.DMA

    def body(feats, coords, cell_ids, recip, kvec, w_in, w_out, kfilt, spread, cotan):
        atoms, chan = feats.shape
        depth = kfilt.shape[0]
        cells = recip.shape[1]
        shape = jax.ShapeDtypeStruct
        height, width = chan // n_dp, 2 * chan + depth
        part = depth // 2
        spread = spread.reshape(1, chan)

        def far(*arrays):
            return [pltpu.with_memory_space_constraint(a, pltpu.HBM) for a in arrays]

        def held(*arrays):
            return [pltpu.VMEM(a.shape, a.dtype) for a in arrays]

        cs, ct, proj, back, shapes, kf, meta = pl.pallas_call(
            functools.partial(gather_kernel, n_ka),
            out_shape=(
                shape((2 * POINTS, atoms), BF16),
                shape((atoms, 2 * POINTS), BF16),
                shape((atoms, chan), BF16),
                shape((atoms, chan), F32),
                shape((cells, POINTS, chan), F32),
                shape((POINTS, chan), F32),
                shape((1, 128), jnp.int32),
            ),
            in_specs=[hbm] * 10,
            out_specs=[vmem] * 7,
            scratch_shapes=held(feats, coords, cell_ids, recip, kvec, w_in, kfilt, spread, cotan, w_out) + [
                pltpu.VMEM((n_ka, 2, part + 16, chan), BF16),
                pltpu.VMEM((n_ka, 2, part, chan), BF16),
                dma((10,)), dma((2, 2, n_ka)), dma((2, 2, n_ka)), dma((2, 2, n_ka)), dma((2, 2, n_ka)),
            ],
            compiler_params=pltpu.CompilerParams(collective_id=0, has_side_effects=True, vmem_limit_bytes=GATHER_VMEM),
            name="gather",
        )(*far(feats, coords, cell_ids, recip, kvec, w_in, kfilt, spread, cotan, w_out))
        act, upd, rsum = pl.pallas_call(
            cell_kernel,
            out_shape=(shape((atoms, chan), BF16), shape((atoms, chan), BF16), shape((POINTS, chan), F32)),
            in_specs=[smem] + [vmem] * 6,
            out_specs=[vmem] * 3,
            scratch_shapes=[
                pltpu.VMEM((2 * POINTS, chan), F32),
                pltpu.VMEM((2 * POINTS, chan), F32),
                pltpu.VMEM((atoms, chan), BF16),
            ],
            compiler_params=pltpu.CompilerParams(vmem_limit_bytes=24 << 20),
            name="cells",
        )(meta, cs, ct, proj, back, shapes, kf)
        results = pl.pallas_call(
            functools.partial(reduce_kernel, n_dp, n_ka, 1.0 / (2 * chan * chan), 1.0 / (depth * n_ka * chan)),
            out_shape=(
                shape((atoms, chan), BF16), shape((atoms, chan), BF16),
                shape((chan, chan), F32), shape((chan, chan), F32), shape((depth, chan), F32),
            ),
            in_specs=[vmem] * 3 + [hbm] * 5,
            out_specs=[vmem] * 5,
            scratch_shapes=held(feats, cotan, w_in, w_out, kvec) + [
                pltpu.VMEM((n_dp, height, width), BF16),
                pltpu.VMEM((n_dp - 1, height, width), BF16),
                pltpu.VMEM((n_dp, height, width), BF16),
                pltpu.VMEM((height, depth), F32),
                pltpu.VMEM((n_ka - 1, height, depth), F32),
                pltpu.VMEM((n_dp, height, depth), F32),
                dma((5,)), dma((n_dp,)), dma((n_dp,)), dma((n_dp,)), dma((n_dp,)),
                dma((n_ka,)), dma((n_ka,)), dma((n_dp,)), dma((n_dp,)),
            ],
            compiler_params=pltpu.CompilerParams(collective_id=1, has_side_effects=True, vmem_limit_bytes=REDUCE_VMEM),
            name="reduce",
        )(act, upd, rsum, feats, cotan, w_in, w_out, kvec)
        return tuple(pl.pallas_call(
            put_kernel,
            out_shape=[shape(r.shape, r.dtype) for r in results],
            in_specs=[vmem] * 5,
            out_specs=[hbm] * 5,
            scratch_shapes=[dma((5,))],
            compiler_params=pltpu.CompilerParams(vmem_limit_bytes=16 << 20),
            name="put",
        )(*results))

    placed = (
        P("dp", None), P(None, "dp"), P("dp", None), P("dp", None, None), P(None, "ka"),
        P(), P(), P("ka", None), P(), P("dp", None),
    )
    return jax.shard_map(
        body,
        mesh=mesh,
        in_specs=placed,
        out_specs=(P("dp", None), P("dp", None), P(), P(), P("ka", None)),
        check_vma=False,
    )
```

profile of v0, /device:TPU:1, one launch (start us, length us, event | category | flops | bytes accessed | tf_op | source)
XLA Modules:
  0.0 68.6 jit_solution(2629868934358647320)
XLA Ops:
  0.6 25.4 %gather.1 = (bf16[768,2048]{1,0:T(8,128)(2,1)S(1)}, bf16[2048,768]{1,0:T(8,128)(2,1)S(1)}, bf16[2048,256]{1,0:T(8,128)(2,1)S(1)}, f32[2048,256]{1,0:T(8,128)S(1)...) custom-call(bf16[2048,256]{1,0:T(8,128)(2,1)} %feats_in.3, f32[3,2048]{1,0:T(4,128)} %coords_in.1, ...), custom_call_target="tpu_custom_call" | custom-call | tf_op jit(solution)/shard_map/gather/pallas_call | solution.py:393
  26.1 0.0 copy-start
  26.1 0.0 copy-start.1
  26.1 0.0 copy-start.2
  26.1 0.0 copy-start.3
  26.1 0.0 copy-start.4
  26.1 15.1 %cells.1 = (bf16[2048,256]{1,0:T(8,128)(2,1)S(1)}, bf16[2048,256]{1,0:T(8,128)(2,1)S(1)}, f32[384,256]{1,0:T(8,128)S(1)}) custom-call(s32[1,128]{1,0:T(1,128)S(1)} %get-tuple-element.20.meta, bf16[768,2048]{1,0:T(8,128)(2,1)S(1)} %get-tuple-element.21.cs, bf16[2048,768]{1,0:T(8,128)(2,1)S(1)} %get-tuple-element.22.ct, ...), custom_call_target="tpu_custom_call" | custom-call | tf_op jit(solution)/shard_map/cells/pallas_call | solution.py:414
  41.2 0.0 copy-done
  41.2 0.0 copy-done.1
  41.2 0.0 copy-done.2
  41.2 0.0 copy-done.3
  41.2 0.0 copy-done.4
  41.3 25.6 %reduce.1 = (bf16[2048,256]{1,0:T(8,128)(2,1)S(1)}, bf16[2048,256]{1,0:T(8,128)(2,1)S(1)}, f32[256,256]{1,0:T(8,128)S(1)}, f32[256,256]{1,0:T(8,128)S(1)}, f32[128,256]{1,0:T(8,128)S(1)}) custom-call(bf16[2048,256]{1,0:T(8,128)(2,1)S(1)} %get-tuple-element.27.act, bf16[2048,256]{1,0:T(8,128)(2,1)S(1)} %get-tuple-element.28.upd, ...), custom_call_target="tpu_custom_call" | custom-call | tf_op jit(solution)/shard_map/reduce/pallas_call | solution.py:427
  66.9 1.6 %put.1 = (bf16[2048,256]{1,0:T(8,128)(2,1)}, bf16[2048,256]{1,0:T(8,128)(2,1)}, f32[256,256]{1,0:T(8,128)}, f32[256,256]{1,0:T(8,128)}, f32[128,256]{1,0:T(8,128)}) custom-call(bf16[2048,256]{1,0:T(8,128)(2,1)S(1)} %get-tuple-element.30.refs_0_, bf16[2048,256]{1,0:T(8,128)(2,1)S(1)} %get-tuple-element.31.refs_1_, f32[256,256]{1,0:T(8,128)S(1)} %get-tuple-element.32.refs_2_, ...), custom_call_target="tpu_custom_call" | custom-call | tf_op jit(solution)/shard_map/put/pallas_call | solution.py:448
Async XLA Ops:
  26.1 15.1 %copy-start = (bf16[2048,256]{1,0:T(8,128)(2,1)S(1)}, bf16[2048,256]{1,0:T(8,128)(2,1)}, u32[]{:S(2)}) copy-start(bf16[2048,256]{1,0:T(8,128)(2,1)} %feats_in.3) | copy-start | bytes 3145732
  26.1 15.1 %copy-start.1 = (bf16[2048,256]{1,0:T(8,128)(2,1)S(1)}, bf16[2048,256]{1,0:T(8,128)(2,1)}, u32[]{:S(2)}) copy-start(bf16[2048,256]{1,0:T(8,128)(2,1)} %cotan_in.3) | copy-start | bytes 3145732
  26.1 15.1 %copy-start.2 = (bf16[256,256]{1,0:T(8,128)(2,1)S(1)}, bf16[256,256]{1,0:T(8,128)(2,1)}, u32[]{:S(2)}) copy-start(bf16[256,256]{1,0:T(8,128)(2,1)} %w_in_in.3) | copy-start | bytes 393220
  26.1 15.1 %copy-start.3 = (bf16[256,256]{1,0:T(8,128)(2,1)S(1)}, bf16[256,256]{1,0:T(8,128)(2,1)}, u32[]{:S(2)}) copy-start(bf16[256,256]{1,0:T(8,128)(2,1)} %w_out_in.3) | copy-start | bytes 393220
  26.1 15.1 %copy-start.4 = (s32[3,128]{1,0:T(4,128)S(1)}, s32[3,128]{1,0:T(4,128)}, u32[]{:S(2)}) copy-start(s32[3,128]{1,0:T(4,128)} %kvec_in.3) | copy-start | bytes 4612
where the time goes:
time: 68.7 us; the launch traced here: 68.6 us
  Pallas kernels  67.6 us (98%)
  between operations  0.9 us (1%)
    pallas_call x1, Pallas kernels, body(): pl.pallas_call(functools.partial(reduce_kernel, n_dp, n_ka, 1.0 / (2 * ch...  25.6 us
    pallas_call x1, Pallas kernels, body(): pl.pallas_call(functools.partial(gather_kernel, n_ka), out_shape=(shape((...  25.4 us
    pallas_call x1, Pallas kernels, body(): pl.pallas_call(cell_kernel, out_shape=(shape((atoms, chan), BF16), shape(...  15.1 us
    pallas_call x1, Pallas kernels, body(): pl.pallas_call(put_kernel, out_shape=[shape(r.shape, r.dtype) for r in re...  1.56 us

commit v1 on v0

--- a/solution.py
+++ b/solution.py
@@ -11,10 +11,11 @@
 F32, BF16 = jnp.float32, jnp.bfloat16
 NT = (((1,), (1,)), ((), ()))
 TN = (((0,), (0,)), ((), ()))
-GATHER_VMEM, REDUCE_VMEM = 30 << 20, 30 << 20
+GATHER_VMEM, REDUCE_VMEM = 30 << 20, 24 << 20
 POINTS = 384
-DEPTHS = (256, 384, 512, 768, 1152)
-HEIGHTS = (96, 160, 224, 320, 528, 784, 1040)
+DEPTHS = (256, 512, 768, 1152)
+PIECES = {544: 2, 1040: 5}
+HEIGHTS = (112, 176, 240, 320, 544, 1040)
 COS = (0.9999992251396179, -19.738981246948242, 64.92865753173828, -85.27162170410156, 58.79049301147461, -21.07110595703125)
 SIN = (6.283185005187988, -41.341590881347656, 81.59994506835938, -76.61447143554688, 41.3428840637207, -12.471243858337402)
 
@@ -123,7 +124,6 @@
             cs[pl.ds(POINTS + at, 16), here] = (turn * poly(SIN, s)).astype(BF16)
 
     chunks = POINTS // 16
-    split = chunks // 2
 
     def envelope():
         loading[3].wait()
@@ -148,29 +148,56 @@
             shapes[i] = jnp.exp(-(q[:, i:i + 1] * spread[...])) * (1.0 / count)
         meta[...] = info
 
+    pending, shared = [], []
+
+    def ways(step):
+        return [way for way in (0, 1) if 0 <= step < hops[way]]
+
+    def slots_of(step):
+        return [lax.rem(me + n_ka - step - 1, n_ka) if way == 0 else lax.rem(me + step + 1, n_ka) for way in ways(step)]
+
+    def arrived(step):
+        for half in (0, 1):
+            for way in ways(step - 1):
+                share(half, way, step - 1).wait_recv()
+
+    def filter_of(slots):
+        point = lax.broadcasted_iota(jnp.int32, (POINTS, 2 * depth), 0).astype(F32)
+        total = None
+        for z in slots:
+            k = jnp.concatenate([high[z, h, part:part + 16, 0:depth] for h in (0, 1)], axis=1).astype(F32)
+            hot = (point == point_of(k)).astype(BF16)
+            terms = jnp.concatenate([high[z, 0, 0:part, :], low[z, 0], high[z, 1, 0:part, :], low[z, 1]], axis=0)
+            new = mm(hot, terms)
+            total = new if total is None else total + new
+        if len(slots) == 1:
+            kf[...] = total
+        else:
+            kf[...] += total
+
     def stage(step):
         if step == 0:
             loading[4].wait()
             loading[5].wait()
             proj[...] = mm(feats[...], w_in[...]).astype(BF16)
             loading[2].wait()
-            pl.loop(0, split)(trig)
+            pl.loop(0, 10)(trig)
         elif step == 1:
-            pl.loop(split, chunks)(trig)
+            filter_of([me])
+            pl.loop(10, 21)(trig)
         elif step == 2:
+            pl.loop(21, chunks)(trig)
             envelope()
             loading[8].wait()
             loading[9].wait()
             back[...] = mm_nt(cotan[...], w_out[...])
         else:
+            arrived(1)
+            filter_of(slots_of(0))
             for p in range(0, 2 * POINTS, 256):
                 for a in range(0, atoms, 256):
                     ct[a:a + 256, p:p + 256] = cs[p:p + 256, a:a + 256].T
 
-    pending, shared = [], []
-
-    def ways(step):
-        return [way for way in (0, 1) if 0 <= step < hops[way]]
 
     for step in range(hops[0] + 1):
         for half in (0, 1):
@@ -186,21 +213,14 @@
                 shared.append(c)
         if step < hops[0]:
             stage(step)
-    for c in shared:
-        c.wait_recv()
-    point = lax.broadcasted_iota(jnp.int32, (POINTS, 2 * depth), 0).astype(F32)
-    total = jnp.zeros((POINTS, chan), F32)
-    for z in range(n_ka):
-        k = jnp.concatenate([high[z, h, part:part + 16, 0:depth] for h in (0, 1)], axis=1).astype(F32)
-        hot = (point == point_of(k)).astype(BF16)
-        terms = jnp.concatenate([high[z, 0, 0:part, :], low[z, 0], high[z, 1, 0:part, :], low[z, 1]], axis=0)
-        total = total + mm(hot, terms)
-    kf[...] = total
+    for step in (2, 3, 4):
+        arrived(step)
+    filter_of(slots_of(1) + slots_of(2) + slots_of(3))
     for c in pending + shared:
         c.wait_send()
 
 
-def cell_kernel(meta, cs, ct, proj, back, shapes, kf, act, upd, rsum, pull, push, grad):
+def cell_kernel(meta, cs, ct, proj, back, shapes, kf, act, upd, pushes, pulls, grad, weights):
     atoms = cs.shape[1]
     half, other = pl.ds(0, POINTS), pl.ds(POINTS, POINTS)
 
@@ -219,47 +239,49 @@
 
     def factors(source, target, i):
         def run(here, inside):
-            picked = jnp.where(inside, source[here, :].astype(F32), 0.0).astype(BF16)
-            target[...] = mm(cs[:, here], picked)
+            rows = source[here, :]
+            picked = jnp.where(inside, rows, jnp.zeros_like(rows))
+            total = mm(cs[:, here], picked)
+            target[...] = total
+            filt = shapes[i] * kf[...]
+            weights[half] = (filt * total[0:POINTS]).astype(BF16)
+            weights[other] = (filt * total[POINTS:]).astype(BF16)
         windows(i, 128, DEPTHS, run)
 
-    def fields(filt, terms, i, use):
-        weights = jnp.concatenate([(filt * terms[half]).astype(BF16), (filt * terms[other]).astype(BF16)], axis=0)
-
+    def fields(i, use):
         def run(here, inside):
-            use(here, inside, mm(ct[here, :], weights))
+            size = inside.shape[0]
+            pieces = PIECES.get(size, 1)
+            for n in range(pieces):
+                at, step = n * (size // pieces), size // pieces
+                rows = pl.ds(pl.multiple_of(here.start + at, 16), step)
+                use(rows, inside[at:at + step], mm(ct[rows, :], weights[...]))
         windows(i, 16, HEIGHTS, run)
 
     def keep(target, here, inside, new):
-        target[here, :] = jnp.where(inside, new, target[here, :].astype(F32)).astype(BF16)
+        target[here, :] = jnp.where(inside, new.astype(BF16), target[here, :])
 
     def forward(here, inside, m):
         s = 0.5 * jnp.tanh(0.5 * m) + 0.5
-        keep(act, here, inside, m * s)
-        keep(grad, here, inside, back[here, :] * (s * (1.0 + m * (1.0 - s))))
-
-    rsum[...] = jnp.zeros_like(rsum)
+        value = m * s
+        keep(act, here, inside, value)
+        keep(grad, here, inside, back[here, :] * (s + value * (1.0 - s)))
 
     @pl.loop(0, shapes.shape[0])
     def _(i):
+        push, pull = pushes.at[i], pulls.at[i]
         factors(proj, push, i)
-        fields(shapes[i] * kf[...], push, i, forward)
+        fields(i, forward)
         factors(grad, pull, i)
-        shape = shapes[i]
-        rsum[...] += shape * (push[half] * pull[half] + push[other] * pull[other])
-        fields(shape * kf[...], pull, i, functools.partial(keep, upd))
+        fields(i, functools.partial(keep, upd))
 
 
 def reduce_kernel(
-    n_dp, n_ka, mean_weights, mean_filter, act, upd, rsum, feats_in, cotan_in, w_in_in, w_out_in, kvec_in,
+    n_dp, n_ka, mean_weights, mean_filter, act, upd, pushes, pulls, shapes, feats, cotan, w_in, w_out, kvec,
     mixed, feat_grad, grad_in, grad_out, grad_filt,
-    feats, cotan, w_in, w_out, kvec, raw, landed, gath, squares, sq_landed, sq_gath,
-    loads, s_send, s_recv, g_send, g_recv, z_send, z_recv, q_send, q_recv,
+    filt, filt_landed, filt_gath, raw, landed, gath, squares, sq_landed, sq_gath,
+    f_send, f_recv, h_send, h_recv, s_send, s_recv, g_send, g_recv, z_send, z_recv, q_send, q_recv,
 ):
-    pairs = ((cotan_in, cotan), (feats_in, feats), (kvec_in, kvec), (w_out_in, w_out), (w_in_in, w_in))
-    loading = [pltpu.make_async_copy(a, b, loads.at[i]) for i, (a, b) in enumerate(pairs)]
-    for c in loading:
-        c.start()
     me, ka = lax.axis_index("dp"), lax.axis_index("ka")
     chan = grad_in.shape[0]
     height = chan // n_dp
@@ -276,87 +298,99 @@
     def _(i):
         pl.semaphore_signal(barrier, inc=1, device_id={"ka": lax.rem(ka + i, n_ka)}, device_id_type=MESH)
 
+    def scatter(source, target, sends, receives):
+        return lambda i: pltpu.make_async_remote_copy(
+            src_ref=source.at[peer(i)], dst_ref=target.at[i - 1], send_sem=sends.at[i - 1], recv_sem=receives.at[i - 1],
+            device_id={"dp": peer(i)}, device_id_type=MESH,
+        )
+
+    def gather(ref, sends, receives):
+        return lambda i: pltpu.make_async_remote_copy(
+            src_ref=ref.at[me], dst_ref=ref.at[me], send_sem=sends.at[i - 1], recv_sem=receives.at[i - 1],
+            device_id={"dp": peer(i)}, device_id_type=MESH,
+        )
+
+    def across(i):
+        return pltpu.make_async_remote_copy(
+            src_ref=squares, dst_ref=sq_landed.at[i - 1], send_sem=z_send.at[i - 1], recv_sem=z_recv.at[i - 1],
+            device_id={"ka": lax.rem(ka + i, n_ka)}, device_id_type=MESH,
+        )
+
+    scatter_filt = scatter(filt, filt_landed, f_send, f_recv)
+    gather_filt = gather(filt_gath, h_send, h_recv)
+    scatter_raw = scatter(raw, landed, s_send, s_recv)
+    gather_raw = gather(gath, g_send, g_recv)
+    gather_sq = gather(sq_gath, q_send, q_recv)
+
+    def each(copy, act_on, n):
+        @pl.loop(1, n)
+        def _(i):
+            act_on(copy(i))
+
+    def start(c):
+        c.start()
+
+    def wait_recv(c):
+        c.wait_recv()
+
+    def wait_send(c):
+        c.wait_send()
+
+    def added(own, others):
+        total = own.astype(F32)
+        for i in range(others.shape[0]):
+            total = total + others[i].astype(F32)
+        return total
+
     atoms, depth = act.shape[0], kvec.shape[1]
-    for c in loading:
-        c.wait()
-    raw[:, :, 0:chan] = mm_tn(act[...], cotan[...]).reshape(n_dp, height, chan).astype(BF16)
-    raw[:, :, chan:2 * chan] = mm_tn(feats[...], upd[...]).reshape(n_dp, height, chan).astype(BF16)
     point = lax.broadcasted_iota(jnp.int32, (POINTS, depth), 0).astype(F32)
     hot = (point == point_of(kvec[...].astype(F32))).astype(BF16).T
-    rest = rsum[...]
+    half, other = pl.ds(0, POINTS), pl.ds(POINTS, POINTS)
+    rest = jnp.zeros((POINTS, chan), F32)
+    for i in range(shapes.shape[0]):
+        rest = rest + shapes[i] * (pushes[i, half] * pulls[i, half] + pushes[i, other] * pulls[i, other])
     own = jnp.zeros((depth, chan), F32)
     for _ in range(3):
         piece = rest.astype(BF16)
         own = own + mm(hot, piece)
         rest = rest - piece.astype(F32)
     own = jnp.concatenate([own[:, 0:chan // 2], own[:, chan // 2:]], axis=0)
-    raw[:, :, 2 * chan:] = own.reshape(n_dp, height, chan // 2).astype(BF16)
+    filt[...] = own.reshape(n_dp, height, chan // 2).astype(BF16)
     pl.semaphore_wait(barrier, n_dp - 1 + n_ka - 1)
-
-    def scatter(i):
-        return pltpu.make_async_remote_copy(
-            src_ref=raw.at[peer(i)], dst_ref=landed.at[i - 1], send_sem=s_send.at[i - 1], recv_sem=s_recv.at[i - 1],
-            device_id={"dp": peer(i)}, device_id_type=MESH,
-        )
-
-    def gather(i):
-        return pltpu.make_async_remote_copy(
-            src_ref=gath.at[me], dst_ref=gath.at[me], send_sem=g_send.at[i - 1], recv_sem=g_recv.at[i - 1],
-            device_id={"dp": peer(i)}, device_id_type=MESH,
-        )
-
-    def across(i):
-        return pltpu.make_async_remote_copy(
-            src_ref=squares, dst_ref=sq_landed.at[i - 1], send_sem=z_send.at[i - 1], recv_sem=z_recv.at[i - 1],
-            device_id={"ka": lax.rem(ka + i, n_ka)}, device_id_type=MESH,
-        )
-
-    def gather_sq(i):
-        return pltpu.make_async_remote_copy(
-            src_ref=sq_gath.at[me], dst_ref=sq_gath.at[me], send_sem=q_send.at[i - 1], recv_sem=q_recv.at[i - 1],
-            device_id={"dp": peer(i)}, device_id_type=MESH,
-        )
-
-    def each(copy, act, n):
-        @pl.loop(1, n)
-        def _(i):
-            act(copy(i))
-
-    each(scatter, lambda c: c.start(), n_dp)
+    each(scatter_filt, start, n_dp)
+    raw[:, :, 0:chan] = mm_tn(act[...], cotan[...]).reshape(n_dp, height, chan).astype(BF16)
+    raw[:, :, chan:2 * chan] = mm_tn(feats[...], upd[...]).reshape(n_dp, height, chan).astype(BF16)
+    each(scatter_raw, start, n_dp)
     for a in range(0, atoms, 512):
         mixed[a:a + 512, :] = (feats[a:a + 512, :].astype(F32) + mm(act[a:a + 512, :], w_out[...])).astype(BF16)
-    each(scatter, lambda c: c.wait_recv(), n_dp)
-    total = raw[me].astype(F32)
-    for i in range(n_dp - 1):
-        total = total + landed[i].astype(F32)
-    gath[me] = total.astype(BF16)
-    each(gather, lambda c: c.start(), n_dp)
-    tail = total[:, 2 * chan:]
-    squares[...] = tail * tail
-    each(across, lambda c: c.start(), n_ka)
+    each(scatter_filt, wait_recv, n_dp)
+    total = added(filt[me], filt_landed)
+    squares[...] = jnp.sum(total * total, axis=0, keepdims=True)
+    each(across, start, n_ka)
+    filt_gath[me] = total.astype(BF16)
+    each(gather_filt, start, n_dp)
+    each(scatter_raw, wait_recv, n_dp)
+    gath[me] = added(raw[me], landed).astype(BF16)
+    each(gather_raw, start, n_dp)
+    each(across, wait_recv, n_ka)
+    sq_gath[me] = added(squares[...], sq_landed)
+    each(gather_sq, start, n_dp)
     for a in range(0, atoms, 512):
         feat_grad[a:a + 512, :] = (cotan[a:a + 512, :].astype(F32) + mm_nt(upd[a:a + 512, :], w_in[...])).astype(BF16)
-    each(across, lambda c: c.wait_recv(), n_ka)
-    added = squares[...]
-    for i in range(n_ka - 1):
-        added = added + sq_landed[i]
-    sq_gath[me] = added
-    each(gather_sq, lambda c: c.start(), n_dp)
-    each(gather, lambda c: c.wait_recv(), n_dp)
-    everything = gath[...].astype(F32).reshape(chan, gath.shape[2])
-    weights = everything[:, 0:2 * chan]
+    each(gather_filt, wait_recv, n_dp)
+    each(gather_sq, wait_recv, n_dp)
+    summed = sq_gath[...].reshape(n_dp, sq_gath.shape[2])
+    scale = lax.rsqrt(jnp.sum(summed, axis=(0, 1), keepdims=True) * mean_filter + 1e-06)
+    tail = filt_gath[...].astype(F32).reshape(chan, chan // 2) * scale
+    grad_filt[...] = jnp.concatenate([tail[0:depth], tail[depth:]], axis=1)
+    each(gather_raw, wait_recv, n_dp)
+    weights = gath[...].astype(F32).reshape(chan, 2 * chan)
     scale = lax.rsqrt(jnp.sum(weights * weights, axis=(0, 1), keepdims=True) * mean_weights + 1e-06)
-    grad_out[...] = everything[:, 0:chan] * scale
-    grad_in[...] = everything[:, chan:2 * chan] * scale
-    each(gather_sq, lambda c: c.wait_recv(), n_dp)
-    summed = sq_gath[...].reshape(n_dp * height, sq_gath.shape[2])
-    scale = lax.rsqrt(jnp.sum(summed, axis=(0, 1), keepdims=True) * mean_filter + 1e-06)
-    tail = everything[:, 2 * chan:] * scale
-    grad_filt[...] = jnp.concatenate([tail[0:depth], tail[depth:]], axis=1)
-    each(scatter, lambda c: c.wait_send(), n_dp)
-    each(gather, lambda c: c.wait_send(), n_dp)
-    each(across, lambda c: c.wait_send(), n_ka)
-    each(gather_sq, lambda c: c.wait_send(), n_dp)
+    grad_out[...] = weights[:, 0:chan] * scale
+    grad_in[...] = weights[:, chan:] * scale
+    for c in (scatter_filt, gather_filt, scatter_raw, gather_raw, gather_sq):
+        each(c, wait_send, n_dp)
+    each(across, wait_send, n_ka)
 
 
 def put_kernel(*refs):
@@ -380,7 +414,7 @@
         depth = kfilt.shape[0]
         cells = recip.shape[1]
         shape = jax.ShapeDtypeStruct
-        height, width = chan // n_dp, 2 * chan + depth
+        height = chan // n_dp
         part = depth // 2
         spread = spread.reshape(1, chan)
 
@@ -411,17 +445,18 @@
             compiler_params=pltpu.CompilerParams(collective_id=0, has_side_effects=True, vmem_limit_bytes=GATHER_VMEM),
             name="gather",
         )(*far(feats, coords, cell_ids, recip, kvec, w_in, kfilt, spread, cotan, w_out))
-        act, upd, rsum = pl.pallas_call(
+        act, upd, pushes, pulls = pl.pallas_call(
             cell_kernel,
-            out_shape=(shape((atoms, chan), BF16), shape((atoms, chan), BF16), shape((POINTS, chan), F32)),
+            out_shape=(
+                shape((atoms, chan), BF16),
+                shape((atoms, chan), BF16),
+                shape((cells, 2 * POINTS, chan), F32),
+                shape((cells, 2 * POINTS, chan), F32),
+            ),
             in_specs=[smem] + [vmem] * 6,
-            out_specs=[vmem] * 3,
-            scratch_shapes=[
-                pltpu.VMEM((2 * POINTS, chan), F32),
-                pltpu.VMEM((2 * POINTS, chan), F32),
-                pltpu.VMEM((atoms, chan), BF16),
-            ],
-            compiler_params=pltpu.CompilerParams(vmem_limit_bytes=24 << 20),
+            out_specs=[vmem] * 4,
+            scratch_shapes=[pltpu.VMEM((atoms, chan), BF16), pltpu.VMEM((2 * POINTS, chan), BF16)],
+            compiler_params=pltpu.CompilerParams(vmem_limit_bytes=16 << 20),
             name="cells",
         )(meta, cs, ct, proj, back, shapes, kf)
         results = pl.pallas_call(
@@ -430,21 +465,22 @@
                 shape((atoms, chan), BF16), shape((atoms, chan), BF16),
                 shape((chan, chan), F32), shape((chan, chan), F32), shape((depth, chan), F32),
             ),
-            in_specs=[vmem] * 3 + [hbm] * 5,
+            in_specs=[vmem] * 10,
             out_specs=[vmem] * 5,
-            scratch_shapes=held(feats, cotan, w_in, w_out, kvec) + [
-                pltpu.VMEM((n_dp, height, width), BF16),
-                pltpu.VMEM((n_dp - 1, height, width), BF16),
-                pltpu.VMEM((n_dp, height, width), BF16),
-                pltpu.VMEM((height, depth), F32),
-                pltpu.VMEM((n_ka - 1, height, depth), F32),
-                pltpu.VMEM((n_dp, height, depth), F32),
-                dma((5,)), dma((n_dp,)), dma((n_dp,)), dma((n_dp,)), dma((n_dp,)),
-                dma((n_ka,)), dma((n_ka,)), dma((n_dp,)), dma((n_dp,)),
-            ],
+            scratch_shapes=[
+                pltpu.VMEM((n_dp, height, chan // 2), BF16),
+                pltpu.VMEM((n_dp - 1, height, chan // 2), BF16),
+                pltpu.VMEM((n_dp, height, chan // 2), BF16),
+                pltpu.VMEM((n_dp, height, 2 * chan), BF16),
+                pltpu.VMEM((n_dp - 1, height, 2 * chan), BF16),
+                pltpu.VMEM((n_dp, height, 2 * chan), BF16),
+                pltpu.VMEM((1, chan // 2), F32),
+                pltpu.VMEM((n_ka - 1, 1, chan // 2), F32),
+                pltpu.VMEM((n_dp, 1, chan // 2), F32),
+            ] + [dma((n_dp,))] * 8 + [dma((n_ka,))] * 2 + [dma((n_dp,))] * 2,
             compiler_params=pltpu.CompilerParams(collective_id=1, has_side_effects=True, vmem_limit_bytes=REDUCE_VMEM),
             name="reduce",
-        )(act, upd, rsum, feats, cotan, w_in, w_out, kvec)
+        )(act, upd, pushes, pulls, shapes, feats, cotan, w_in, w_out, kvec)
         return tuple(pl.pallas_call(
             put_kernel,
             out_shape=[shape(r.shape, r.dtype) for r in results],

time: 68.7 us -> 65.3 us (0.951)
  Pallas kernels: 67.6 us -> 64.4 us
    pallas_call x1, Pallas kernels: 15.1 us -> 13.2 us  [body(): pl.pallas_call(cell_kernel, out_shape=(shape((atoms, chan), BF16), shape(...]
    pallas_call x1, Pallas kernels: 25.6 us -> 24.5 us  [body(): pl.pallas_call(functools.partial(reduce_kernel, n_dp, n_ka, 1.0 / (2 * ch...]
where the time goes in v1:
time: 65.3 us
  Pallas kernels  64.4 us (99%)
  between operations  0.9 us (1%)
    pallas_call x1, Pallas kernels, body(): pl.pallas_call(functools.partial(gather_kernel, n_ka), out_shape=(shape((...  25.1 us
    pallas_call x1, Pallas kernels, body(): pl.pallas_call(functools.partial(reduce_kernel, n_dp, n_ka, 1.0 / (2 * ch...  24.5 us
    pallas_call x1, Pallas kernels, body(): pl.pallas_call(cell_kernel, out_shape=(shape((atoms, chan), BF16), shape(...  13.2 us
    pallas_call x1, Pallas kernels, body(): pl.pallas_call(put_kernel, out_shape=[shape(r.shape, r.dtype) for r in re...  1.56 us

profile of v1, /device:TPU:1, one launch (start us, length us, event | category | flops | bytes accessed | tf_op | source)
XLA Modules:
  0.0 65.3 jit_solution(13453469619265441431)
XLA Ops:
  0.6 25.1 %gather.1 = (bf16[768,2048]{1,0:T(8,128)(2,1)S(1)}, bf16[2048,768]{1,0:T(8,128)(2,1)S(1)}, bf16[2048,256]{1,0:T(8,128)(2,1)S(1)}, f32[2048,256]{1,0:T(8,128)S(1)...) custom-call(bf16[2048,256]{1,0:T(8,128)(2,1)} %feats.1, f32[3,2048]{1,0:T(4,128)} %coords_in.1, ...), custom_call_target="tpu_custom_call" | custom-call | tf_op jit(solution)/shard_map/gather/pallas_call | solution.py:427
  25.8 0.0 copy-start
  25.8 0.0 copy-start.1
  25.8 0.0 copy-start.2
  25.8 0.0 copy-start.3
  25.8 0.0 copy-start.4
  25.8 13.2 %cells.1 = (bf16[2048,256]{1,0:T(8,128)(2,1)S(1)}, bf16[2048,256]{1,0:T(8,128)(2,1)S(1)}, f32[8,768,256]{2,1,0:T(8,128)S(1)}, f32[8,768,256]{2,1,0:T(8,128)S(1)}) custom-call(s32[1,128]{1,0:T(1,128)S(1)} %get-tuple-element.21.meta, bf16[768,2048]{1,0:T(8,128)(2,1)S(1)} %get-tuple-element.22.cs, bf16[2048,768]{1,0:T(8,128)(2,1)S(1)} %get-tuple-element.23.ct, ...), custom_call_target="tpu_custom_call" | custom-call | tf_op jit(solution)/shard_map/cells/pallas_call | solution.py:448
  39.0 0.0 copy-done
  39.0 0.0 copy-done.1
  39.0 0.0 copy-done.2
  39.0 0.0 copy-done.3
  39.1 0.0 copy-done.4
  39.1 24.5 %reduce.1 = (bf16[2048,256]{1,0:T(8,128)(2,1)S(1)}, bf16[2048,256]{1,0:T(8,128)(2,1)S(1)}, f32[256,256]{1,0:T(8,128)S(1)}, f32[256,256]{1,0:T(8,128)S(1)}, f32[128,256]{1,0:T(8,128)S(1)}) custom-call(bf16[2048,256]{1,0:T(8,128)(2,1)S(1)} %get-tuple-element.28.act, bf16[2048,256]{1,0:T(8,128)(2,1)S(1)} %get-tuple-element.29.upd, ...), custom_call_target="tpu_custom_call" | custom-call | tf_op jit(solution)/shard_map/reduce/pallas_call | solution.py:462
  63.6 1.6 %put.1 = (bf16[2048,256]{1,0:T(8,128)(2,1)}, bf16[2048,256]{1,0:T(8,128)(2,1)}, f32[256,256]{1,0:T(8,128)}, f32[256,256]{1,0:T(8,128)}, f32[128,256]{1,0:T(8,128)}) custom-call(bf16[2048,256]{1,0:T(8,128)(2,1)S(1)} %get-tuple-element.32.refs_0_, bf16[2048,256]{1,0:T(8,128)(2,1)S(1)} %get-tuple-element.33.refs_1_, f32[256,256]{1,0:T(8,128)S(1)} %get-tuple-element.34.refs_2_, ...), custom_call_target="tpu_custom_call" | custom-call | tf_op jit(solution)/shard_map/put/pallas_call | solution.py:484
Async XLA Ops:
  25.8 13.3 %copy-start = (bf16[2048,256]{1,0:T(8,128)(2,1)S(1)}, bf16[2048,256]{1,0:T(8,128)(2,1)}, u32[]{:S(2)}) copy-start(bf16[2048,256]{1,0:T(8,128)(2,1)} %feats.1) | copy-start | bytes 3145732
  25.8 13.3 %copy-start.1 = (bf16[2048,256]{1,0:T(8,128)(2,1)S(1)}, bf16[2048,256]{1,0:T(8,128)(2,1)}, u32[]{:S(2)}) copy-start(bf16[2048,256]{1,0:T(8,128)(2,1)} %cotan.1) | copy-start | bytes 3145732
  25.8 13.3 %copy-start.2 = (bf16[256,256]{1,0:T(8,128)(2,1)S(1)}, bf16[256,256]{1,0:T(8,128)(2,1)}, u32[]{:S(2)}) copy-start(bf16[256,256]{1,0:T(8,128)(2,1)} %w_in.1) | copy-start | bytes 393220
  25.8 13.3 %copy-start.3 = (bf16[256,256]{1,0:T(8,128)(2,1)S(1)}, bf16[256,256]{1,0:T(8,128)(2,1)}, u32[]{:S(2)}) copy-start(bf16[256,256]{1,0:T(8,128)(2,1)} %w_out.1) | copy-start | bytes 393220
  25.8 13.3 %copy-start.4 = (s32[3,128]{1,0:T(4,128)S(1)}, s32[3,128]{1,0:T(4,128)}, u32[]{:S(2)}) copy-start(s32[3,128]{1,0:T(4,128)} %kvec.1) | copy-start | bytes 4612

commit v2 on v0

--- a/solution.py
+++ b/solution.py
@@ -11,10 +11,11 @@
 F32, BF16 = jnp.float32, jnp.bfloat16
 NT = (((1,), (1,)), ((), ()))
 TN = (((0,), (0,)), ((), ()))
-GATHER_VMEM, REDUCE_VMEM = 30 << 20, 30 << 20
+GATHER_VMEM, REDUCE_VMEM = 30 << 20, 24 << 20
 POINTS = 384
-DEPTHS = (256, 384, 512, 768, 1152)
-HEIGHTS = (96, 160, 224, 320, 528, 784, 1040)
+DEPTHS = (256, 512, 768, 1152)
+PIECES = {544: 2, 1040: 5}
+HEIGHTS = (112, 176, 240, 320, 544, 1040)
 COS = (0.9999992251396179, -19.738981246948242, 64.92865753173828, -85.27162170410156, 58.79049301147461, -21.07110595703125)
 SIN = (6.283185005187988, -41.341590881347656, 81.59994506835938, -76.61447143554688, 41.3428840637207, -12.471243858337402)
 
@@ -78,13 +79,13 @@
     loading[1].wait()
     first = kfilt[...].astype(BF16)
     second = (kfilt[...] - first.astype(F32)).astype(BF16)
-    kpad = jnp.concatenate([kvec[...].astype(F32), jnp.zeros((13, depth), F32)], axis=0)
+    kpad = jnp.concatenate([kvec[...].astype(F32), jnp.zeros((5, depth), F32)], axis=0)
     for h in range(2):
         rows = slice(h * part, (h + 1) * part)
         high[me, h, 0:part, :] = first[rows]
         low[me, h] = second[rows]
         k = kpad[:, rows]
-        high[me, h, part:part + 16, :] = jnp.concatenate([k, k, k, k], axis=1).astype(BF16)
+        high[me, h, part:part + 8, :] = jnp.concatenate([k, k, k, k], axis=1).astype(BF16)
     pl.semaphore_wait(barrier, 3)
 
     hops = (n_ka // 2, n_ka - 1 - n_ka // 2)
@@ -123,7 +124,6 @@
             cs[pl.ds(POINTS + at, 16), here] = (turn * poly(SIN, s)).astype(BF16)
 
     chunks = POINTS // 16
-    split = chunks // 2
 
     def envelope():
         loading[3].wait()
@@ -148,29 +148,58 @@
             shapes[i] = jnp.exp(-(q[:, i:i + 1] * spread[...])) * (1.0 / count)
         meta[...] = info
 
+    pending, shared = [], []
+
+    def ways(step):
+        return [way for way in (0, 1) if 0 <= step < hops[way]]
+
+    def slots_of(step):
+        return [lax.rem(me + n_ka - step - 1, n_ka) if way == 0 else lax.rem(me + step + 1, n_ka) for way in ways(step)]
+
+    def arrived(step):
+        for half in (0, 1):
+            for way in ways(step - 1):
+                share(half, way, step - 1).wait_recv()
+
+    def filter_of(slots, begin=False):
+        point = lax.broadcasted_iota(jnp.int32, (POINTS, 2 * depth), 0).astype(F32)
+        total = None
+        for z in slots:
+            k = jnp.concatenate([high[z, h, part:part + 8, 0:depth] for h in (0, 1)], axis=1).astype(F32)
+            hot = (point == point_of(k)).astype(BF16)
+            terms = jnp.concatenate([high[z, 0, 0:part, :], low[z, 0], high[z, 1, 0:part, :], low[z, 1]], axis=0)
+            new = mm(hot, terms)
+            total = new if total is None else total + new
+        if begin:
+            kf[...] = total
+        else:
+            kf[...] += total
+
     def stage(step):
         if step == 0:
             loading[4].wait()
             loading[5].wait()
             proj[...] = mm(feats[...], w_in[...]).astype(BF16)
             loading[2].wait()
-            pl.loop(0, split)(trig)
+            pl.loop(0, 10)(trig)
         elif step == 1:
-            pl.loop(split, chunks)(trig)
+            filter_of([me], True)
+            pl.loop(10, 21)(trig)
         elif step == 2:
+            pl.loop(21, chunks)(trig)
             envelope()
             loading[8].wait()
             loading[9].wait()
             back[...] = mm_nt(cotan[...], w_out[...])
         else:
+            arrived(1)
+            filter_of(slots_of(0))
             for p in range(0, 2 * POINTS, 256):
                 for a in range(0, atoms, 256):
                     ct[a:a + 256, p:p + 256] = cs[p:p + 256, a:a + 256].T
-
-    pending, shared = [], []
-
-    def ways(step):
-        return [way for way in (0, 1) if 0 <= step < hops[way]]
+            arrived(2)
+            filter_of(slots_of(1))
+
 
     for step in range(hops[0] + 1):
         for half in (0, 1):
@@ -186,21 +215,14 @@
                 shared.append(c)
         if step < hops[0]:
             stage(step)
-    for c in shared:
-        c.wait_recv()
-    point = lax.broadcasted_iota(jnp.int32, (POINTS, 2 * depth), 0).astype(F32)
-    total = jnp.zeros((POINTS, chan), F32)
-    for z in range(n_ka):
-        k = jnp.concatenate([high[z, h, part:part + 16, 0:depth] for h in (0, 1)], axis=1).astype(F32)
-        hot = (point == point_of(k)).astype(BF16)
-        terms = jnp.concatenate([high[z, 0, 0:part, :], low[z, 0], high[z, 1, 0:part, :], low[z, 1]], axis=0)
-        total = total + mm(hot, terms)
-    kf[...] = total
+    for step in (3, 4):
+        arrived(step)
+        filter_of(slots_of(step - 1))
     for c in pending + shared:
         c.wait_send()
 
 
-def cell_kernel(meta, cs, ct, proj, back, shapes, kf, act, upd, rsum, pull, push, grad):
+def cell_kernel(meta, cs, ct, proj, back, shapes, kf, act, upd, pushes, pulls, grad, weights):
     atoms = cs.shape[1]
     half, other = pl.ds(0, POINTS), pl.ds(POINTS, POINTS)
 
@@ -219,47 +241,49 @@
 
     def factors(source, target, i):
         def run(here, inside):
-            picked = jnp.where(inside, source[here, :].astype(F32), 0.0).astype(BF16)
-            target[...] = mm(cs[:, here], picked)
+            rows = source[here, :]
+            picked = jnp.where(inside, rows, jnp.zeros_like(rows))
+            total = mm(cs[:, here], picked)
+            target[...] = total
+            filt = shapes[i] * kf[...]
+            weights[half] = (filt * total[0:POINTS]).astype(BF16)
+            weights[other] = (filt * total[POINTS:]).astype(BF16)
         windows(i, 128, DEPTHS, run)
 
-    def fields(filt, terms, i, use):
-        weights = jnp.concatenate([(filt * terms[half]).astype(BF16), (filt * terms[other]).astype(BF16)], axis=0)
-
+    def fields(i, use):
         def run(here, inside):
-            use(here, inside, mm(ct[here, :], weights))
+            size = inside.shape[0]
+            pieces = PIECES.get(size, 1)
+            for n in range(pieces):
+                at, step = n * (size // pieces), size // pieces
+                rows = pl.ds(pl.multiple_of(here.start + at, 16), step)
+                use(rows, inside[at:at + step], mm(ct[rows, :], weights[...]))
         windows(i, 16, HEIGHTS, run)
 
     def keep(target, here, inside, new):
-        target[here, :] = jnp.where(inside, new, target[here, :].astype(F32)).astype(BF16)
+        target[here, :] = jnp.where(inside, new.astype(BF16), target[here, :])
 
     def forward(here, inside, m):
         s = 0.5 * jnp.tanh(0.5 * m) + 0.5
-        keep(act, here, inside, m * s)
-        keep(grad, here, inside, back[here, :] * (s * (1.0 + m * (1.0 - s))))
-
-    rsum[...] = jnp.zeros_like(rsum)
+        value = m * s
+        keep(act, here, inside, value)
+        keep(grad, here, inside, back[here, :] * (s + value * (1.0 - s)))
 
     @pl.loop(0, shapes.shape[0])
     def _(i):
+        push, pull = pushes.at[i], pulls.at[i]
         factors(proj, push, i)
-        fields(shapes[i] * kf[...], push, i, forward)
+        fields(i, forward)
         factors(grad, pull, i)
-        shape = shapes[i]
-        rsum[...] += shape * (push[half] * pull[half] + push[other] * pull[other])
-        fields(shape * kf[...], pull, i, functools.partial(keep, upd))
+        fields(i, functools.partial(keep, upd))
 
 
 def reduce_kernel(
-    n_dp, n_ka, mean_weights, mean_filter, act, upd, rsum, feats_in, cotan_in, w_in_in, w_out_in, kvec_in,
+    n_dp, n_ka, mean_weights, mean_filter, act, upd, pushes, pulls, shapes, feats, cotan, w_in, w_out, kvec,
     mixed, feat_grad, grad_in, grad_out, grad_filt,
-    feats, cotan, w_in, w_out, kvec, raw, landed, gath, squares, sq_landed, sq_gath,
-    loads, s_send, s_recv, g_send, g_recv, z_send, z_recv, q_send, q_recv,
+    raw, landed, gath, squares, sq_landed, sq_gath,
+    s_send, s_recv, g_send, g_recv, z_send, z_recv, q_send, q_recv,
 ):
-    pairs = ((cotan_in, cotan), (feats_in, feats), (kvec_in, kvec), (w_out_in, w_out), (w_in_in, w_in))
-    loading = [pltpu.make_async_copy(a, b, loads.at[i]) for i, (a, b) in enumerate(pairs)]
-    for c in loading:
-        c.start()
     me, ka = lax.axis_index("dp"), lax.axis_index("ka")
     chan = grad_in.shape[0]
     height = chan // n_dp
@@ -277,15 +301,16 @@
         pl.semaphore_signal(barrier, inc=1, device_id={"ka": lax.rem(ka + i, n_ka)}, device_id_type=MESH)
 
     atoms, depth = act.shape[0], kvec.shape[1]
-    for c in loading:
-        c.wait()
     raw[:, :, 0:chan] = mm_tn(act[...], cotan[...]).reshape(n_dp, height, chan).astype(BF16)
     raw[:, :, chan:2 * chan] = mm_tn(feats[...], upd[...]).reshape(n_dp, height, chan).astype(BF16)
     point = lax.broadcasted_iota(jnp.int32, (POINTS, depth), 0).astype(F32)
     hot = (point == point_of(kvec[...].astype(F32))).astype(BF16).T
-    rest = rsum[...]
+    half, other = pl.ds(0, POINTS), pl.ds(POINTS, POINTS)
+    rest = jnp.zeros((POINTS, chan), F32)
+    for i in range(shapes.shape[0]):
+        rest = rest + shapes[i] * (pushes[i, half] * pulls[i, half] + pushes[i, other] * pulls[i, other])
     own = jnp.zeros((depth, chan), F32)
-    for _ in range(3):
+    for _ in range(2):
         piece = rest.astype(BF16)
         own = own + mm(hot, piece)
         rest = rest - piece.astype(F32)
@@ -330,10 +355,10 @@
     for i in range(n_dp - 1):
         total = total + landed[i].astype(F32)
     gath[me] = total.astype(BF16)
+    tail = total[:, 2 * chan:]
+    squares[...] = jnp.sum(tail * tail, axis=0, keepdims=True)
+    each(across, lambda c: c.start(), n_ka)
     each(gather, lambda c: c.start(), n_dp)
-    tail = total[:, 2 * chan:]
-    squares[...] = tail * tail
-    each(across, lambda c: c.start(), n_ka)
     for a in range(0, atoms, 512):
         feat_grad[a:a + 512, :] = (cotan[a:a + 512, :].astype(F32) + mm_nt(upd[a:a + 512, :], w_in[...])).astype(BF16)
     each(across, lambda c: c.wait_recv(), n_ka)
@@ -349,7 +374,7 @@
     grad_out[...] = everything[:, 0:chan] * scale
     grad_in[...] = everything[:, chan:2 * chan] * scale
     each(gather_sq, lambda c: c.wait_recv(), n_dp)
-    summed = sq_gath[...].reshape(n_dp * height, sq_gath.shape[2])
+    summed = sq_gath[...].reshape(n_dp, sq_gath.shape[2])
     scale = lax.rsqrt(jnp.sum(summed, axis=(0, 1), keepdims=True) * mean_filter + 1e-06)
     tail = everything[:, 2 * chan:] * scale
     grad_filt[...] = jnp.concatenate([tail[0:depth], tail[depth:]], axis=1)
@@ -404,24 +429,25 @@
             in_specs=[hbm] * 10,
             out_specs=[vmem] * 7,
             scratch_shapes=held(feats, coords, cell_ids, recip, kvec, w_in, kfilt, spread, cotan, w_out) + [
-                pltpu.VMEM((n_ka, 2, part + 16, chan), BF16),
+                pltpu.VMEM((n_ka, 2, part + 8, chan), BF16),
                 pltpu.VMEM((n_ka, 2, part, chan), BF16),
                 dma((10,)), dma((2, 2, n_ka)), dma((2, 2, n_ka)), dma((2, 2, n_ka)), dma((2, 2, n_ka)),
             ],
             compiler_params=pltpu.CompilerParams(collective_id=0, has_side_effects=True, vmem_limit_bytes=GATHER_VMEM),
             name="gather",
         )(*far(feats, coords, cell_ids, recip, kvec, w_in, kfilt, spread, cotan, w_out))
-        act, upd, rsum = pl.pallas_call(
+        act, upd, pushes, pulls = pl.pallas_call(
             cell_kernel,
-            out_shape=(shape((atoms, chan), BF16), shape((atoms, chan), BF16), shape((POINTS, chan), F32)),
+            out_shape=(
+                shape((atoms, chan), BF16),
+                shape((atoms, chan), BF16),
+                shape((cells, 2 * POINTS, chan), F32),
+                shape((cells, 2 * POINTS, chan), F32),
+            ),
             in_specs=[smem] + [vmem] * 6,
-            out_specs=[vmem] * 3,
-            scratch_shapes=[
-                pltpu.VMEM((2 * POINTS, chan), F32),
-                pltpu.VMEM((2 * POINTS, chan), F32),
-                pltpu.VMEM((atoms, chan), BF16),
-            ],
-            compiler_params=pltpu.CompilerParams(vmem_limit_bytes=24 << 20),
+            out_specs=[vmem] * 4,
+            scratch_shapes=[pltpu.VMEM((atoms, chan), BF16), pltpu.VMEM((2 * POINTS, chan), BF16)],
+            compiler_params=pltpu.CompilerParams(vmem_limit_bytes=16 << 20),
             name="cells",
         )(meta, cs, ct, proj, back, shapes, kf)
         results = pl.pallas_call(
@@ -430,21 +456,19 @@
                 shape((atoms, chan), BF16), shape((atoms, chan), BF16),
                 shape((chan, chan), F32), shape((chan, chan), F32), shape((depth, chan), F32),
             ),
-            in_specs=[vmem] * 3 + [hbm] * 5,
+            in_specs=[vmem] * 10,
             out_specs=[vmem] * 5,
-            scratch_shapes=held(feats, cotan, w_in, w_out, kvec) + [
+            scratch_shapes=[
                 pltpu.VMEM((n_dp, height, width), BF16),
                 pltpu.VMEM((n_dp - 1, height, width), BF16),
                 pltpu.VMEM((n_dp, height, width), BF16),
-                pltpu.VMEM((height, depth), F32),
-                pltpu.VMEM((n_ka - 1, height, depth), F32),
-                pltpu.VMEM((n_dp, height, depth), F32),
-                dma((5,)), dma((n_dp,)), dma((n_dp,)), dma((n_dp,)), dma((n_dp,)),
-                dma((n_ka,)), dma((n_ka,)), dma((n_dp,)), dma((n_dp,)),
-            ],
+                pltpu.VMEM((1, depth), F32),
+                pltpu.VMEM((n_ka - 1, 1, depth), F32),
+                pltpu.VMEM((n_dp, 1, depth), F32),
+            ] + [dma((n_dp,))] * 4 + [dma((n_ka,))] * 2 + [dma((n_dp,))] * 2,
             compiler_params=pltpu.CompilerParams(collective_id=1, has_side_effects=True, vmem_limit_bytes=REDUCE_VMEM),
             name="reduce",
-        )(act, upd, rsum, feats, cotan, w_in, w_out, kvec)
+        )(act, upd, pushes, pulls, shapes, feats, cotan, w_in, w_out, kvec)
         return tuple(pl.pallas_call(
             put_kernel,
             out_shape=[shape(r.shape, r.dtype) for r in results],

time: 68.7 us -> 64.1 us (0.933)
  Pallas kernels: 67.6 us -> 63 us
    pallas_call x1, Pallas kernels: 15.1 us -> 13.1 us  [body(): pl.pallas_call(cell_kernel, out_shape=(shape((atoms, chan), BF16), shape(...]
    pallas_call x1, Pallas kernels: 25.6 us -> 23.7 us  [body(): pl.pallas_call(functools.partial(reduce_kernel, n_dp, n_ka, 1.0 / (2 * ch...]
    pallas_call x1, Pallas kernels: 25.4 us -> 24.6 us  [body(): pl.pallas_call(functools.partial(gather_kernel, n_ka), out_shape=(shape((...]
where the time goes in v2:
time: 64.1 us; the launch traced here: 63.9 us
  Pallas kernels  63 us (98%)
  between operations  0.9 us (1%)
    pallas_call x1, Pallas kernels, body(): pl.pallas_call(functools.partial(gather_kernel, n_ka), out_shape=(shape((...  24.6 us
    pallas_call x1, Pallas kernels, body(): pl.pallas_call(functools.partial(reduce_kernel, n_dp, n_ka, 1.0 / (2 * ch...  23.7 us
    pallas_call x1, Pallas kernels, body(): pl.pallas_call(cell_kernel, out_shape=(shape((atoms, chan), BF16), shape(...  13.1 us
    pallas_call x1, Pallas kernels, body(): pl.pallas_call(put_kernel, out_shape=[shape(r.shape, r.dtype) for r in re...  1.56 us

profile of v2, /device:TPU:1, one launch (start us, length us, event | category | flops | bytes accessed | tf_op | source)
XLA Modules:
  0.0 63.9 jit_solution(42832207833660965)
XLA Ops:
  0.6 24.6 %gather.1 = (bf16[768,2048]{1,0:T(8,128)(2,1)S(1)}, bf16[2048,768]{1,0:T(8,128)(2,1)S(1)}, bf16[2048,256]{1,0:T(8,128)(2,1)S(1)}, f32[2048,256]{1,0:T(8,128)S(1)...) custom-call(bf16[2048,256]{1,0:T(8,128)(2,1)} %feats.1, f32[3,2048]{1,0:T(4,128)} %coords_in.1, ...), custom_call_target="tpu_custom_call" | custom-call | tf_op jit(solution)/shard_map/gather/pallas_call | solution.py:418
  25.3 0.0 copy-start
  25.3 0.0 copy-start.1
  25.3 0.0 copy-start.2
  25.3 0.0 copy-start.3
  25.3 0.0 copy-start.4
  25.3 13.1 %cells.1 = (bf16[2048,256]{1,0:T(8,128)(2,1)S(1)}, bf16[2048,256]{1,0:T(8,128)(2,1)S(1)}, f32[8,768,256]{2,1,0:T(8,128)S(1)}, f32[8,768,256]{2,1,0:T(8,128)S(1)}) custom-call(s32[1,128]{1,0:T(1,128)S(1)} %get-tuple-element.21.meta, bf16[768,2048]{1,0:T(8,128)(2,1)S(1)} %get-tuple-element.22.cs, bf16[2048,768]{1,0:T(8,128)(2,1)S(1)} %get-tuple-element.23.ct, ...), custom_call_target="tpu_custom_call" | custom-call | tf_op jit(solution)/shard_map/cells/pallas_call | solution.py:439
  38.4 0.0 copy-done
  38.5 0.0 copy-done.1
  38.5 0.0 copy-done.2
  38.5 0.0 copy-done.3
  38.5 0.0 copy-done.4
  38.5 23.7 %reduce.1 = (bf16[2048,256]{1,0:T(8,128)(2,1)S(1)}, bf16[2048,256]{1,0:T(8,128)(2,1)S(1)}, f32[256,256]{1,0:T(8,128)S(1)}, f32[256,256]{1,0:T(8,128)S(1)}, f32[128,256]{1,0:T(8,128)S(1)}) custom-call(bf16[2048,256]{1,0:T(8,128)(2,1)S(1)} %get-tuple-element.28.act, bf16[2048,256]{1,0:T(8,128)(2,1)S(1)} %get-tuple-element.29.upd, ...), custom_call_target="tpu_custom_call" | custom-call | tf_op jit(solution)/shard_map/reduce/pallas_call | solution.py:453
  62.2 1.6 %put.1 = (bf16[2048,256]{1,0:T(8,128)(2,1)}, bf16[2048,256]{1,0:T(8,128)(2,1)}, f32[256,256]{1,0:T(8,128)}, f32[256,256]{1,0:T(8,128)}, f32[128,256]{1,0:T(8,128)}) custom-call(bf16[2048,256]{1,0:T(8,128)(2,1)S(1)} %get-tuple-element.32.refs_0_, bf16[2048,256]{1,0:T(8,128)(2,1)S(1)} %get-tuple-element.33.refs_1_, f32[256,256]{1,0:T(8,128)S(1)} %get-tuple-element.34.refs_2_, ...), custom_call_target="tpu_custom_call" | custom-call | tf_op jit(solution)/shard_map/put/pallas_call | solution.py:472
Async XLA Ops:
  25.3 13.2 %copy-start = (bf16[2048,256]{1,0:T(8,128)(2,1)S(1)}, bf16[2048,256]{1,0:T(8,128)(2,1)}, u32[]{:S(2)}) copy-start(bf16[2048,256]{1,0:T(8,128)(2,1)} %feats.1) | copy-start | bytes 3145732
  25.3 13.2 %copy-start.1 = (bf16[2048,256]{1,0:T(8,128)(2,1)S(1)}, bf16[2048,256]{1,0:T(8,128)(2,1)}, u32[]{:S(2)}) copy-start(bf16[2048,256]{1,0:T(8,128)(2,1)} %cotan.1) | copy-start | bytes 3145732
  25.3 13.2 %copy-start.2 = (bf16[256,256]{1,0:T(8,128)(2,1)S(1)}, bf16[256,256]{1,0:T(8,128)(2,1)}, u32[]{:S(2)}) copy-start(bf16[256,256]{1,0:T(8,128)(2,1)} %w_in.1) | copy-start | bytes 393220
  25.3 13.2 %copy-start.3 = (bf16[256,256]{1,0:T(8,128)(2,1)S(1)}, bf16[256,256]{1,0:T(8,128)(2,1)}, u32[]{:S(2)}) copy-start(bf16[256,256]{1,0:T(8,128)(2,1)} %w_out.1) | copy-start | bytes 393220
  25.3 13.2 %copy-start.4 = (s32[3,128]{1,0:T(4,128)S(1)}, s32[3,128]{1,0:T(4,128)}, u32[]{:S(2)}) copy-start(s32[3,128]{1,0:T(4,128)} %kvec.1) | copy-start | bytes 4612

commit v3 on v2

--- a/solution.py
+++ b/solution.py
@@ -222,7 +222,7 @@
         c.wait_send()
 
 
-def cell_kernel(meta, cs, ct, proj, back, shapes, kf, act, upd, pushes, pulls, grad, weights):
+def cell_kernel(meta, cs, ct, proj, back, shapes, kf, act, upd, rsum, grad, weights, push):
     atoms = cs.shape[1]
     half, other = pl.ds(0, POINTS), pl.ds(POINTS, POINTS)
 
@@ -239,13 +239,14 @@
                 run(pl.ds(start, size), (row >= off) & (row < off + n))
             low = size
 
-    def factors(source, target, i):
+    def factors(source, i, use):
         def run(here, inside):
             rows = source[here, :]
             picked = jnp.where(inside, rows, jnp.zeros_like(rows))
             total = mm(cs[:, here], picked)
-            target[...] = total
-            filt = shapes[i] * kf[...]
+            shape = shapes[i]
+            use(shape, total)
+            filt = shape * kf[...]
             weights[half] = (filt * total[0:POINTS]).astype(BF16)
             weights[other] = (filt * total[POINTS:]).astype(BF16)
         windows(i, 128, DEPTHS, run)
@@ -269,17 +270,24 @@
         keep(act, here, inside, value)
         keep(grad, here, inside, back[here, :] * (s + value * (1.0 - s)))
 
+    def hold(shape, total):
+        push[...] = total
+
+    def add(shape, total):
+        rsum[...] += shape * (push[half] * total[0:POINTS] + push[other] * total[POINTS:])
+
+    rsum[...] = jnp.zeros_like(rsum)
+
     @pl.loop(0, shapes.shape[0])
     def _(i):
-        push, pull = pushes.at[i], pulls.at[i]
-        factors(proj, push, i)
+        factors(proj, i, hold)
         fields(i, forward)
-        factors(grad, pull, i)
+        factors(grad, i, add)
         fields(i, functools.partial(keep, upd))
 
 
 def reduce_kernel(
-    n_dp, n_ka, mean_weights, mean_filter, act, upd, pushes, pulls, shapes, feats, cotan, w_in, w_out, kvec,
+    n_dp, n_ka, mean_weights, mean_filter, act, upd, rsum, feats, cotan, w_in, w_out, kvec,
     mixed, feat_grad, grad_in, grad_out, grad_filt,
     raw, landed, gath, squares, sq_landed, sq_gath,
     s_send, s_recv, g_send, g_recv, z_send, z_recv, q_send, q_recv,
@@ -305,10 +313,7 @@
     raw[:, :, chan:2 * chan] = mm_tn(feats[...], upd[...]).reshape(n_dp, height, chan).astype(BF16)
     point = lax.broadcasted_iota(jnp.int32, (POINTS, depth), 0).astype(F32)
     hot = (point == point_of(kvec[...].astype(F32))).astype(BF16).T
-    half, other = pl.ds(0, POINTS), pl.ds(POINTS, POINTS)
-    rest = jnp.zeros((POINTS, chan), F32)
-    for i in range(shapes.shape[0]):
-        rest = rest + shapes[i] * (pushes[i, half] * pulls[i, half] + pushes[i, other] * pulls[i, other])
+    rest = rsum[...]
     own = jnp.zeros((depth, chan), F32)
     for _ in range(2):
         piece = rest.astype(BF16)
@@ -436,17 +441,20 @@
             compiler_params=pltpu.CompilerParams(collective_id=0, has_side_effects=True, vmem_limit_bytes=GATHER_VMEM),
             name="gather",
         )(*far(feats, coords, cell_ids, recip, kvec, w_in, kfilt, spread, cotan, w_out))
-        act, upd, pushes, pulls = pl.pallas_call(
+        act, upd, rsum = pl.pallas_call(
             cell_kernel,
             out_shape=(
                 shape((atoms, chan), BF16),
                 shape((atoms, chan), BF16),
-                shape((cells, 2 * POINTS, chan), F32),
-                shape((cells, 2 * POINTS, chan), F32),
+                shape((POINTS, chan), F32),
             ),
             in_specs=[smem] + [vmem] * 6,
-            out_specs=[vmem] * 4,
-            scratch_shapes=[pltpu.VMEM((atoms, chan), BF16), pltpu.VMEM((2 * POINTS, chan), BF16)],
+            out_specs=[vmem] * 3,
+            scratch_shapes=[
+                pltpu.VMEM((atoms, chan), BF16),
+                pltpu.VMEM((2 * POINTS, chan), BF16),
+                pltpu.VMEM((2 * POINTS, chan), F32),
+            ],
             compiler_params=pltpu.CompilerParams(vmem_limit_bytes=16 << 20),
             name="cells",
         )(meta, cs, ct, proj, back, shapes, kf)
@@ -456,7 +464,7 @@
                 shape((atoms, chan), BF16), shape((atoms, chan), BF16),
                 shape((chan, chan), F32), shape((chan, chan), F32), shape((depth, chan), F32),
             ),
-            in_specs=[vmem] * 10,
+            in_specs=[vmem] * 8,
             out_specs=[vmem] * 5,
             scratch_shapes=[
                 pltpu.VMEM((n_dp, height, width), BF16),
@@ -468,7 +476,7 @@
             ] + [dma((n_dp,))] * 4 + [dma((n_ka,))] * 2 + [dma((n_dp,))] * 2,
             compiler_params=pltpu.CompilerParams(collective_id=1, has_side_effects=True, vmem_limit_bytes=REDUCE_VMEM),
             name="reduce",
-        )(act, upd, pushes, pulls, shapes, feats, cotan, w_in, w_out, kvec)
+        )(act, upd, rsum, feats, cotan, w_in, w_out, kvec)
         return tuple(pl.pallas_call(
             put_kernel,
             out_shape=[shape(r.shape, r.dtype) for r in results],

time: 64.1 us -> 64.2 us (level)
  no operation moved by 1% of the time
where the time goes in v3:
time: 64.2 us
  Pallas kernels  63.5 us (99%)
  between operations  0.74 us (1%)
    pallas_call x1, Pallas kernels, body(): pl.pallas_call(functools.partial(gather_kernel, n_ka), out_shape=(shape((...  24.6 us
    pallas_call x1, Pallas kernels, body(): pl.pallas_call(functools.partial(reduce_kernel, n_dp, n_ka, 1.0 / (2 * ch...  24 us
    pallas_call x1, Pallas kernels, body(): pl.pallas_call(cell_kernel, out_shape=(shape((atoms, chan), BF16), shape(...  13.3 us
    pallas_call x1, Pallas kernels, body(): pl.pallas_call(put_kernel, out_shape=[shape(r.shape, r.dtype) for r in re...  1.56 us

profile of v3, /device:TPU:1, one launch (start us, length us, event | category | flops | bytes accessed | tf_op | source)
XLA Modules:
  0.0 64.2 jit_solution(15232570990515895717)
XLA Ops:
  0.6 24.6 %gather.1 = (bf16[768,2048]{1,0:T(8,128)(2,1)S(1)}, bf16[2048,768]{1,0:T(8,128)(2,1)S(1)}, bf16[2048,256]{1,0:T(8,128)(2,1)S(1)}, f32[2048,256]{1,0:T(8,128)S(1)...) custom-call(bf16[2048,256]{1,0:T(8,128)(2,1)} %feats.1, f32[3,2048]{1,0:T(4,128)} %coords_in.1, ...), custom_call_target="tpu_custom_call" | custom-call | tf_op jit(solution)/shard_map/gather/pallas_call | solution.py:423
  25.3 0.0 copy-start
  25.3 0.0 copy-start.1
  25.3 0.0 copy-start.2
  25.3 0.0 copy-start.3
  25.3 0.0 copy-start.4
  25.3 13.3 %cells.1 = (bf16[2048,256]{1,0:T(8,128)(2,1)S(1)}, bf16[2048,256]{1,0:T(8,128)(2,1)S(1)}, f32[384,256]{1,0:T(8,128)S(1)}) custom-call(s32[1,128]{1,0:T(1,128)S(1)} %get-tuple-element.20.meta, bf16[768,2048]{1,0:T(8,128)(2,1)S(1)} %get-tuple-element.21.cs, bf16[2048,768]{1,0:T(8,128)(2,1)S(1)} %get-tuple-element.22.ct, ...), custom_call_target="tpu_custom_call" | custom-call | tf_op jit(solution)/shard_map/cells/pallas_call | solution.py:444
  38.6 0.0 copy-done
  38.6 0.0 copy-done.1
  38.6 0.0 copy-done.2
  38.7 0.0 copy-done.3
  38.7 0.0 copy-done.4
  38.7 24.0 %reduce.1 = (bf16[2048,256]{1,0:T(8,128)(2,1)S(1)}, bf16[2048,256]{1,0:T(8,128)(2,1)S(1)}, f32[256,256]{1,0:T(8,128)S(1)}, f32[256,256]{1,0:T(8,128)S(1)}, f32[128,256]{1,0:T(8,128)S(1)}) custom-call(bf16[2048,256]{1,0:T(8,128)(2,1)S(1)} %get-tuple-element.27.act, bf16[2048,256]{1,0:T(8,128)(2,1)S(1)} %get-tuple-element.28.upd, ...), custom_call_target="tpu_custom_call" | custom-call | tf_op jit(solution)/shard_map/reduce/pallas_call | solution.py:461
  62.7 1.6 %put.1 = (bf16[2048,256]{1,0:T(8,128)(2,1)}, bf16[2048,256]{1,0:T(8,128)(2,1)}, f32[256,256]{1,0:T(8,128)}, f32[256,256]{1,0:T(8,128)}, f32[128,256]{1,0:T(8,128)}) custom-call(bf16[2048,256]{1,0:T(8,128)(2,1)S(1)} %get-tuple-element.30.refs_0_, bf16[2048,256]{1,0:T(8,128)(2,1)S(1)} %get-tuple-element.31.refs_1_, f32[256,256]{1,0:T(8,128)S(1)} %get-tuple-element.32.refs_2_, ...), custom_call_target="tpu_custom_call" | custom-call | tf_op jit(solution)/shard_map/put/pallas_call | solution.py:480
Async XLA Ops:
  25.3 13.4 %copy-start = (bf16[2048,256]{1,0:T(8,128)(2,1)S(1)}, bf16[2048,256]{1,0:T(8,128)(2,1)}, u32[]{:S(2)}) copy-start(bf16[2048,256]{1,0:T(8,128)(2,1)} %feats.1) | copy-start | bytes 3145732
  25.3 13.4 %copy-start.1 = (bf16[2048,256]{1,0:T(8,128)(2,1)S(1)}, bf16[2048,256]{1,0:T(8,128)(2,1)}, u32[]{:S(2)}) copy-start(bf16[2048,256]{1,0:T(8,128)(2,1)} %cotan.1) | copy-start | bytes 3145732
  25.3 13.4 %copy-start.2 = (bf16[256,256]{1,0:T(8,128)(2,1)S(1)}, bf16[256,256]{1,0:T(8,128)(2,1)}, u32[]{:S(2)}) copy-start(bf16[256,256]{1,0:T(8,128)(2,1)} %w_in.1) | copy-start | bytes 393220
  25.3 13.4 %copy-start.3 = (bf16[256,256]{1,0:T(8,128)(2,1)S(1)}, bf16[256,256]{1,0:T(8,128)(2,1)}, u32[]{:S(2)}) copy-start(bf16[256,256]{1,0:T(8,128)(2,1)} %w_out.1) | copy-start | bytes 393220
  25.3 13.4 %copy-start.4 = (s32[3,128]{1,0:T(4,128)S(1)}, s32[3,128]{1,0:T(4,128)}, u32[]{:S(2)}) copy-start(s32[3,128]{1,0:T(4,128)} %kvec.1) | copy-start | bytes 4612

commit v4 on v3

--- a/solution.py
+++ b/solution.py
@@ -352,7 +352,8 @@
         def _(i):
             act(copy(i))
 
-    each(scatter, lambda c: c.start(), n_dp)
+    for i in range(1, n_dp):
+        scatter(i).start()
     for a in range(0, atoms, 512):
         mixed[a:a + 512, :] = (feats[a:a + 512, :].astype(F32) + mm(act[a:a + 512, :], w_out[...])).astype(BF16)
     each(scatter, lambda c: c.wait_recv(), n_dp)
@@ -363,7 +364,8 @@
     tail = total[:, 2 * chan:]
     squares[...] = jnp.sum(tail * tail, axis=0, keepdims=True)
     each(across, lambda c: c.start(), n_ka)
-    each(gather, lambda c: c.start(), n_dp)
+    for i in range(1, n_dp):
+        gather(i).start()
     for a in range(0, atoms, 512):
         feat_grad[a:a + 512, :] = (cotan[a:a + 512, :].astype(F32) + mm_nt(upd[a:a + 512, :], w_in[...])).astype(BF16)
     each(across, lambda c: c.wait_recv(), n_ka)

time: 64.2 us -> 64.3 us (level)
  no operation moved by 1% of the time
where the time goes in v4:
time: 64.3 us; the launch traced here: 64.4 us
  Pallas kernels  63.4 us (99%)
  between operations  0.9 us (1%)
    pallas_call x1, Pallas kernels, body(): pl.pallas_call(functools.partial(gather_kernel, n_ka), out_shape=(shape((...  24.6 us
    pallas_call x1, Pallas kernels, body(): pl.pallas_call(functools.partial(reduce_kernel, n_dp, n_ka, 1.0 / (2 * ch...  23.8 us
    pallas_call x1, Pallas kernels, body(): pl.pallas_call(cell_kernel, out_shape=(shape((atoms, chan), BF16), shape(...  13.5 us
    pallas_call x1, Pallas kernels, body(): pl.pallas_call(put_kernel, out_shape=[shape(r.shape, r.dtype) for r in re...  1.56 us

profile of v4, /device:TPU:1, one launch (start us, length us, event | category | flops | bytes accessed | tf_op | source)
XLA Modules:
  0.0 64.4 jit_solution(3139210790546369437)
XLA Ops:
  0.6 24.6 %gather.1 = (bf16[768,2048]{1,0:T(8,128)(2,1)S(1)}, bf16[2048,768]{1,0:T(8,128)(2,1)S(1)}, bf16[2048,256]{1,0:T(8,128)(2,1)S(1)}, f32[2048,256]{1,0:T(8,128)S(1)...) custom-call(bf16[2048,256]{1,0:T(8,128)(2,1)} %feats.1, f32[3,2048]{1,0:T(4,128)} %coords_in.1, ...), custom_call_target="tpu_custom_call" | custom-call | tf_op jit(solution)/shard_map/gather/pallas_call | solution.py:425
  25.3 0.0 copy-start
  25.3 0.0 copy-start.1
  25.3 0.0 copy-start.2
  25.3 0.0 copy-start.3
  25.3 0.0 copy-start.4
  25.3 13.5 %cells.1 = (bf16[2048,256]{1,0:T(8,128)(2,1)S(1)}, bf16[2048,256]{1,0:T(8,128)(2,1)S(1)}, f32[384,256]{1,0:T(8,128)S(1)}) custom-call(s32[1,128]{1,0:T(1,128)S(1)} %get-tuple-element.20.meta, bf16[768,2048]{1,0:T(8,128)(2,1)S(1)} %get-tuple-element.21.cs, bf16[2048,768]{1,0:T(8,128)(2,1)S(1)} %get-tuple-element.22.ct, ...), custom_call_target="tpu_custom_call" | custom-call | tf_op jit(solution)/shard_map/cells/pallas_call | solution.py:446
  38.8 0.0 copy-done
  38.8 0.0 copy-done.1
  38.8 0.0 copy-done.2
  38.8 0.0 copy-done.3
  38.8 0.0 copy-done.4
  38.8 23.8 %reduce.1 = (bf16[2048,256]{1,0:T(8,128)(2,1)S(1)}, bf16[2048,256]{1,0:T(8,128)(2,1)S(1)}, f32[256,256]{1,0:T(8,128)S(1)}, f32[256,256]{1,0:T(8,128)S(1)}, f32[128,256]{1,0:T(8,128)S(1)}) custom-call(bf16[2048,256]{1,0:T(8,128)(2,1)S(1)} %get-tuple-element.27.act, bf16[2048,256]{1,0:T(8,128)(2,1)S(1)} %get-tuple-element.28.upd, ...), custom_call_target="tpu_custom_call" | custom-call | tf_op jit(solution)/shard_map/reduce/pallas_call | solution.py:463
  62.6 1.6 %put.1 = (bf16[2048,256]{1,0:T(8,128)(2,1)}, bf16[2048,256]{1,0:T(8,128)(2,1)}, f32[256,256]{1,0:T(8,128)}, f32[256,256]{1,0:T(8,128)}, f32[128,256]{1,0:T(8,128)}) custom-call(bf16[2048,256]{1,0:T(8,128)(2,1)S(1)} %get-tuple-element.30.refs_0_, bf16[2048,256]{1,0:T(8,128)(2,1)S(1)} %get-tuple-element.31.refs_1_, f32[256,256]{1,0:T(8,128)S(1)} %get-tuple-element.32.refs_2_, ...), custom_call_target="tpu_custom_call" | custom-call | tf_op jit(solution)/shard_map/put/pallas_call | solution.py:482
Async XLA Ops:
  25.3 13.5 %copy-start = (bf16[2048,256]{1,0:T(8,128)(2,1)S(1)}, bf16[2048,256]{1,0:T(8,128)(2,1)}, u32[]{:S(2)}) copy-start(bf16[2048,256]{1,0:T(8,128)(2,1)} %feats.1) | copy-start | bytes 3145732
  25.3 13.5 %copy-start.1 = (bf16[2048,256]{1,0:T(8,128)(2,1)S(1)}, bf16[2048,256]{1,0:T(8,128)(2,1)}, u32[]{:S(2)}) copy-start(bf16[2048,256]{1,0:T(8,128)(2,1)} %cotan.1) | copy-start | bytes 3145732
  25.3 13.5 %copy-start.2 = (bf16[256,256]{1,0:T(8,128)(2,1)S(1)}, bf16[256,256]{1,0:T(8,128)(2,1)}, u32[]{:S(2)}) copy-start(bf16[256,256]{1,0:T(8,128)(2,1)} %w_in.1) | copy-start | bytes 393220
  25.3 13.5 %copy-start.3 = (bf16[256,256]{1,0:T(8,128)(2,1)S(1)}, bf16[256,256]{1,0:T(8,128)(2,1)}, u32[]{:S(2)}) copy-start(bf16[256,256]{1,0:T(8,128)(2,1)} %w_out.1) | copy-start | bytes 393220
  25.3 13.5 %copy-start.4 = (s32[3,128]{1,0:T(4,128)S(1)}, s32[3,128]{1,0:T(4,128)}, u32[]{:S(2)}) copy-start(s32[3,128]{1,0:T(4,128)} %kvec.1) | copy-start | bytes 4612
